TPU v7x, 256 devices: a whole 4x4x8 slice. The times are simulated.
256 devices in a mesh: ctx: 32 (over x, y, core), head: 8 (over z).
Axes of the slice: x: 4, y: 4, z: 8, core: 2. Of those that a mesh axis runs over, the one named last changes fastest.
Arguments:
- features: bfloat16 [16384, 8192], P('ctx', 'head'), may hold values from -6 to 6
- gate_values: bfloat16 [16384, 8192], P('ctx', 'head'), may hold values from -6 to 6
- write_proj: bfloat16 [16384, 1024], P('ctx', 'head'), may hold values from -0.0234375 to 0.0234375
- read_proj: bfloat16 [16384, 1024], P('ctx', 'head'), may hold values from -6 to 6
- step_size: float32 [128, 16384], P('head', 'ctx'), may hold values from 0.25 to 2
- log_decay: float32 [128, 16384], P('head', 'ctx'), may hold values from -1 to 0
- starts: int32 [16384], P('ctx'), may hold values from 0 to 1
- skip_weight: float32 [128], P('head'), may hold values from 0.5 to 1.5
- norm_gain: float32 [8192], P('head'), may hold values from 0.1 to 1.9
- out_weight: bfloat16 [8192, 4096], P('head'), may hold values from -0.0625 to 0.0625
Outputs:
- mixed: bfloat16 [16384, 4096], P(('ctx', 'head'))
All inputs are finite; a program needn't handle non-finite values.
Results may differ from a plain program's by a relative error of at most 0.0061.
Values sent between devices are 32-bit elements; how exact they have to be, the bound alone decides.
A program may use at most 128 MiB of HBM per device.

v0:
```python
import jax
import jax.numpy as jnp
from jax import lax
from jax.sharding import PartitionSpec as P

HEADS = 128
HEAD_DIM = 64
NSTATE = 128
GROUPS = 8
SPAN = 256


eps = 1e-05


def passed_along(value, axis, steps):
    count = lax.axis_size(axis)
    initial, last = (max(0, -steps), min(count, count - steps))
    return lax.ppermute(value, axis, [(source, source + steps) for source in range(initial, last)])


def body(
    features,
    gate_values,
    write_proj,
    read_proj,
    step_size,
    log_decay,
    starts,
    skip_weight,
    norm_gain,
    out_weight,
):
    tokens = features.shape[0]
    heads_dev = step_size.shape[0]
    groups_dev = write_proj.shape[1] // NSTATE
    per_group = HEADS // GROUPS
    blocks = tokens // SPAN
    feat_blocks = features.reshape(blocks, SPAN, heads_dev, HEAD_DIM)
    write_blocks = write_proj.reshape(blocks, SPAN, groups_dev, NSTATE)
    read_blocks = read_proj.reshape(blocks, SPAN, groups_dev, NSTATE)
    step_blocks = step_size.reshape(heads_dev, blocks, SPAN)
    running = jnp.cumsum(log_decay.reshape(heads_dev, blocks, SPAN), axis=2)
    seg_local = jnp.cumsum(starts.reshape(blocks, SPAN), axis=1)
    position = jnp.arange(SPAN)
    causal = position[:, None] >= position[None, :]
    together = (seg_local[:, :, None] == seg_local[:, None, :]) & causal[None]
    spread_log = running[:, :, :, None] - running[:, :, None, :]
    damping = jnp.where(together[None], jnp.exp(jnp.where(together[None], spread_log, 0.0)), 0.0)
    scores = jnp.einsum(
        "kign,kjgn->gkij", read_blocks, write_blocks, preferred_element_type=jnp.float32
    )
    weights = (
        (damping * step_blocks[:, :, None, :]).reshape(groups_dev, per_group, blocks, SPAN, SPAN)
        * scores[:, None]
    ).astype(jnp.bfloat16)
    weights = weights.reshape(heads_dev, blocks, SPAN, SPAN)
    intra_out = jnp.einsum(
        "hkij,kjhp->kihp", weights, feat_blocks, preferred_element_type=jnp.float32
    )
    tail_scale = (
        jnp.where(
            seg_local[None] == seg_local[None, :, -1:], jnp.exp(running[:, :, -1:] - running), 0.0
        )
        * step_blocks
    )
    scaled_in = (tail_scale.transpose(1, 2, 0)[..., None] * feat_blocks.astype(jnp.float32)).astype(
        jnp.bfloat16
    )
    block_states = jnp.einsum(
        "kjgep,kjgn->kgepn",
        scaled_in.reshape(blocks, SPAN, groups_dev, per_group, HEAD_DIM),
        write_blocks,
        preferred_element_type=jnp.float32,
    ).reshape(blocks, heads_dev, HEAD_DIM, NSTATE)
    keep_scale = jnp.where(seg_local[None, :, -1] == 0, jnp.exp(running[:, :, -1]), 0.0)
    total_mult = jnp.ones((heads_dev,), jnp.float32)
    total_state = jnp.zeros((heads_dev, HEAD_DIM, NSTATE), jnp.float32)
    entry_mult = []
    entry_state = []
    for block_id in range(blocks):
        entry_mult.append(total_mult)
        entry_state.append(total_state)
        total_state = keep_scale[:, block_id][:, None, None] * total_state + block_states[block_id]
        total_mult = total_mult * keep_scale[:, block_id]

    def relay_step(index, incoming):
        leaving = total_mult[:, None, None] * incoming + total_state
        return passed_along(leaving, "ctx", 1)

    incoming = lax.fori_loop(0, lax.axis_size("ctx") - 1, relay_step, jnp.zeros_like(total_state))
    carried = jnp.stack(
        [
            entry_mult[block_id][:, None, None] * incoming + entry_state[block_id]
            for block_id in range(blocks)
        ]
    )
    entry_read = carried.astype(jnp.bfloat16)
    carried_out = jnp.einsum(
        "kign,kgepn->kigep",
        read_blocks,
        entry_read.reshape(blocks, groups_dev, per_group, HEAD_DIM, NSTATE),
        preferred_element_type=jnp.float32,
    ).reshape(blocks, SPAN, heads_dev, HEAD_DIM)
    reach_scale = jnp.where(seg_local[None] == 0, jnp.exp(running), 0.0).transpose(1, 2, 0)
    mixed_out = (
        intra_out
        + reach_scale[..., None] * carried_out
        + skip_weight[None, None, :, None] * feat_blocks.astype(jnp.float32)
    )
    gated = mixed_out.reshape(tokens, heads_dev * HEAD_DIM) * jax.nn.silu(
        gate_values.astype(jnp.float32)
    )
    grouped = gated.reshape(tokens, groups_dev, per_group * HEAD_DIM)
    mean_square = jnp.mean(grouped * grouped, axis=-1, keepdims=True)
    normed = (
        (grouped * lax.rsqrt(mean_square + eps)).reshape(tokens, heads_dev * HEAD_DIM)
        * norm_gain[None, :]
    ).astype(jnp.bfloat16)
    summed = lax.psum_scatter(
        jnp.dot(normed, out_weight, preferred_element_type=jnp.float32),
        "head",
        scatter_dimension=0,
        tiled=True,
    )
    return summed.astype(jnp.bfloat16)


def solution(mesh):
    placed = (
        P("ctx", "head"),
        P("ctx", "head"),
        P("ctx", "head"),
        P("ctx", "head"),
        P("head", "ctx"),
        P("head", "ctx"),
        P("ctx"),
        P("head"),
        P("head"),
        P("head", None),
    )
    return jax.shard_map(
        body, mesh=mesh, in_specs=placed, out_specs=P(("ctx", "head"), None), check_vma=False
    )
```

profile of v0, /device:TPU:6, one launch (start us, length us, event | category | flops | bytes accessed | tf_op | source)
XLA Modules:
  0.0 536.7 jit_solution(15123418818422443098)
XLA Ops:
  22.4 394.6 %while.10 = (s32[]{:T(128)}, f32[16,64,128]{2,1,0:T(8,128)S(1)}, f32[16]{0:T(128)S(1)}, f32[16,64,128]{2,1,0:T(8,128)S(1)}, s32[]{:T(128)}) while((s32[]{:T(128)}, f32[16,64,128]{2,1,0:T(8,128)S(1)}, f32[16]{0:T(128)S(1)}, f32[16,64,128]{2,1,0:T(8,128)S(1)}, s32[]{:T(128)}) %tuple.23), condition=%wide.region_5.6_spmd, body=%wide.region_4.5_spmd.sunk | while | flops 262146 | bytes 3670181 | solution.py:91
  24.4 10.7 %collective-permute-done = f32[16,64,128]{2,1,0:T(8,128)S(1)} collective-permute-done((f32[16,64,128]{2,1,0:T(8,128)S(1)}, f32[16,64,128]{2,1,0:T(8,128)S(1)}, u32[]{:S(2)}, u32[]{:S(2)}) %collective-permute-start) | collective-permute-done | bytes 524320 | tf_op jit(solution)/shard_map/while/body/eval_jaxpr/ppermute | solution.py:19
  37.2 10.7 %collective-permute-done = f32[16,64,128]{2,1,0:T(8,128)S(1)} collective-permute-done((f32[16,64,128]{2,1,0:T(8,128)S(1)}, f32[16,64,128]{2,1,0:T(8,128)S(1)}, u32[]{:S(2)}, u32[]{:S(2)}) %collective-permute-start) | collective-permute-done | bytes 524320 | tf_op jit(solution)/shard_map/while/body/eval_jaxpr/ppermute | solution.py:19
  49.9 10.7 %collective-permute-done = f32[16,64,128]{2,1,0:T(8,128)S(1)} collective-permute-done((f32[16,64,128]{2,1,0:T(8,128)S(1)}, f32[16,64,128]{2,1,0:T(8,128)S(1)}, u32[]{:S(2)}, u32[]{:S(2)}) %collective-permute-start) | collective-permute-done | bytes 524320 | tf_op jit(solution)/shard_map/while/body/eval_jaxpr/ppermute | solution.py:19
  62.6 10.7 %collective-permute-done = f32[16,64,128]{2,1,0:T(8,128)S(1)} collective-permute-done((f32[16,64,128]{2,1,0:T(8,128)S(1)}, f32[16,64,128]{2,1,0:T(8,128)S(1)}, u32[]{:S(2)}, u32[]{:S(2)}) %collective-permute-start) | collective-permute-done | bytes 524320 | tf_op jit(solution)/shard_map/while/body/eval_jaxpr/ppermute | solution.py:19
  75.4 10.7 %collective-permute-done = f32[16,64,128]{2,1,0:T(8,128)S(1)} collective-permute-done((f32[16,64,128]{2,1,0:T(8,128)S(1)}, f32[16,64,128]{2,1,0:T(8,128)S(1)}, u32[]{:S(2)}, u32[]{:S(2)}) %collective-permute-start) | collective-permute-done | bytes 524320 | tf_op jit(solution)/shard_map/while/body/eval_jaxpr/ppermute | solution.py:19
  88.1 10.7 %collective-permute-done = f32[16,64,128]{2,1,0:T(8,128)S(1)} collective-permute-done((f32[16,64,128]{2,1,0:T(8,128)S(1)}, f32[16,64,128]{2,1,0:T(8,128)S(1)}, u32[]{:S(2)}, u32[]{:S(2)}) %collective-permute-start) | collective-permute-done | bytes 524320 | tf_op jit(solution)/shard_map/while/body/eval_jaxpr/ppermute | solution.py:19
  100.8 10.7 %collective-permute-done = f32[16,64,128]{2,1,0:T(8,128)S(1)} collective-permute-done((f32[16,64,128]{2,1,0:T(8,128)S(1)}, f32[16,64,128]{2,1,0:T(8,128)S(1)}, u32[]{:S(2)}, u32[]{:S(2)}) %collective-permute-start) | collective-permute-done | bytes 524320 | tf_op jit(solution)/shard_map/while/body/eval_jaxpr/ppermute | solution.py:19
  113.5 10.7 %collective-permute-done = f32[16,64,128]{2,1,0:T(8,128)S(1)} collective-permute-done((f32[16,64,128]{2,1,0:T(8,128)S(1)}, f32[16,64,128]{2,1,0:T(8,128)S(1)}, u32[]{:S(2)}, u32[]{:S(2)}) %collective-permute-start) | collective-permute-done | bytes 524320 | tf_op jit(solution)/shard_map/while/body/eval_jaxpr/ppermute | solution.py:19
  126.3 10.7 %collective-permute-done = f32[16,64,128]{2,1,0:T(8,128)S(1)} collective-permute-done((f32[16,64,128]{2,1,0:T(8,128)S(1)}, f32[16,64,128]{2,1,0:T(8,128)S(1)}, u32[]{:S(2)}, u32[]{:S(2)}) %collective-permute-start) | collective-permute-done | bytes 524320 | tf_op jit(solution)/shard_map/while/body/eval_jaxpr/ppermute | solution.py:19
  139.0 10.7 %collective-permute-done = f32[16,64,128]{2,1,0:T(8,128)S(1)} collective-permute-done((f32[16,64,128]{2,1,0:T(8,128)S(1)}, f32[16,64,128]{2,1,0:T(8,128)S(1)}, u32[]{:S(2)}, u32[]{:S(2)}) %collective-permute-start) | collective-permute-done | bytes 524320 | tf_op jit(solution)/shard_map/while/body/eval_jaxpr/ppermute | solution.py:19
  151.7 10.7 %collective-permute-done = f32[16,64,128]{2,1,0:T(8,128)S(1)} collective-permute-done((f32[16,64,128]{2,1,0:T(8,128)S(1)}, f32[16,64,128]{2,1,0:T(8,128)S(1)}, u32[]{:S(2)}, u32[]{:S(2)}) %collective-permute-start) | collective-permute-done | bytes 524320 | tf_op jit(solution)/shard_map/while/body/eval_jaxpr/ppermute | solution.py:19
  164.5 10.7 %collective-permute-done = f32[16,64,128]{2,1,0:T(8,128)S(1)} collective-permute-done((f32[16,64,128]{2,1,0:T(8,128)S(1)}, f32[16,64,128]{2,1,0:T(8,128)S(1)}, u32[]{:S(2)}, u32[]{:S(2)}) %collective-permute-start) | collective-permute-done | bytes 524320 | tf_op jit(solution)/shard_map/while/body/eval_jaxpr/ppermute | solution.py:19
  177.2 10.7 %collective-permute-done = f32[16,64,128]{2,1,0:T(8,128)S(1)} collective-permute-done((f32[16,64,128]{2,1,0:T(8,128)S(1)}, f32[16,64,128]{2,1,0:T(8,128)S(1)}, u32[]{:S(2)}, u32[]{:S(2)}) %collective-permute-start) | collective-permute-done | bytes 524320 | tf_op jit(solution)/shard_map/while/body/eval_jaxpr/ppermute | solution.py:19
  189.9 10.7 %collective-permute-done = f32[16,64,128]{2,1,0:T(8,128)S(1)} collective-permute-done((f32[16,64,128]{2,1,0:T(8,128)S(1)}, f32[16,64,128]{2,1,0:T(8,128)S(1)}, u32[]{:S(2)}, u32[]{:S(2)}) %collective-permute-start) | collective-permute-done | bytes 524320 | tf_op jit(solution)/shard_map/while/body/eval_jaxpr/ppermute | solution.py:19
  202.7 10.7 %collective-permute-done = f32[16,64,128]{2,1,0:T(8,128)S(1)} collective-permute-done((f32[16,64,128]{2,1,0:T(8,128)S(1)}, f32[16,64,128]{2,1,0:T(8,128)S(1)}, u32[]{:S(2)}, u32[]{:S(2)}) %collective-permute-start) | collective-permute-done | bytes 524320 | tf_op jit(solution)/shard_map/while/body/eval_jaxpr/ppermute | solution.py:19
  215.4 10.7 %collective-permute-done = f32[16,64,128]{2,1,0:T(8,128)S(1)} collective-permute-done((f32[16,64,128]{2,1,0:T(8,128)S(1)}, f32[16,64,128]{2,1,0:T(8,128)S(1)}, u32[]{:S(2)}, u32[]{:S(2)}) %collective-permute-start) | collective-permute-done | bytes 524320 | tf_op jit(solution)/shard_map/while/body/eval_jaxpr/ppermute | solution.py:19
  228.1 10.7 %collective-permute-done = f32[16,64,128]{2,1,0:T(8,128)S(1)} collective-permute-done((f32[16,64,128]{2,1,0:T(8,128)S(1)}, f32[16,64,128]{2,1,0:T(8,128)S(1)}, u32[]{:S(2)}, u32[]{:S(2)}) %collective-permute-start) | collective-permute-done | bytes 524320 | tf_op jit(solution)/shard_map/while/body/eval_jaxpr/ppermute | solution.py:19
  240.8 10.7 %collective-permute-done = f32[16,64,128]{2,1,0:T(8,128)S(1)} collective-permute-done((f32[16,64,128]{2,1,0:T(8,128)S(1)}, f32[16,64,128]{2,1,0:T(8,128)S(1)}, u32[]{:S(2)}, u32[]{:S(2)}) %collective-permute-start) | collective-permute-done | bytes 524320 | tf_op jit(solution)/shard_map/while/body/eval_jaxpr/ppermute | solution.py:19
  253.6 10.7 %collective-permute-done = f32[16,64,128]{2,1,0:T(8,128)S(1)} collective-permute-done((f32[16,64,128]{2,1,0:T(8,128)S(1)}, f32[16,64,128]{2,1,0:T(8,128)S(1)}, u32[]{:S(2)}, u32[]{:S(2)}) %collective-permute-start) | collective-permute-done | bytes 524320 | tf_op jit(solution)/shard_map/while/body/eval_jaxpr/ppermute | solution.py:19
  266.3 10.7 %collective-permute-done = f32[16,64,128]{2,1,0:T(8,128)S(1)} collective-permute-done((f32[16,64,128]{2,1,0:T(8,128)S(1)}, f32[16,64,128]{2,1,0:T(8,128)S(1)}, u32[]{:S(2)}, u32[]{:S(2)}) %collective-permute-start) | collective-permute-done | bytes 524320 | tf_op jit(solution)/shard_map/while/body/eval_jaxpr/ppermute | solution.py:19
  279.0 10.7 %collective-permute-done = f32[16,64,128]{2,1,0:T(8,128)S(1)} collective-permute-done((f32[16,64,128]{2,1,0:T(8,128)S(1)}, f32[16,64,128]{2,1,0:T(8,128)S(1)}, u32[]{:S(2)}, u32[]{:S(2)}) %collective-permute-start) | collective-permute-done | bytes 524320 | tf_op jit(solution)/shard_map/while/body/eval_jaxpr/ppermute | solution.py:19
  291.8 10.7 %collective-permute-done = f32[16,64,128]{2,1,0:T(8,128)S(1)} collective-permute-done((f32[16,64,128]{2,1,0:T(8,128)S(1)}, f32[16,64,128]{2,1,0:T(8,128)S(1)}, u32[]{:S(2)}, u32[]{:S(2)}) %collective-permute-start) | collective-permute-done | bytes 524320 | tf_op jit(solution)/shard_map/while/body/eval_jaxpr/ppermute | solution.py:19
  304.5 10.7 %collective-permute-done = f32[16,64,128]{2,1,0:T(8,128)S(1)} collective-permute-done((f32[16,64,128]{2,1,0:T(8,128)S(1)}, f32[16,64,128]{2,1,0:T(8,128)S(1)}, u32[]{:S(2)}, u32[]{:S(2)}) %collective-permute-start) | collective-permute-done | bytes 524320 | tf_op jit(solution)/shard_map/while/body/eval_jaxpr/ppermute | solution.py:19
  317.2 10.7 %collective-permute-done = f32[16,64,128]{2,1,0:T(8,128)S(1)} collective-permute-done((f32[16,64,128]{2,1,0:T(8,128)S(1)}, f32[16,64,128]{2,1,0:T(8,128)S(1)}, u32[]{:S(2)}, u32[]{:S(2)}) %collective-permute-start) | collective-permute-done | bytes 524320 | tf_op jit(solution)/shard_map/while/body/eval_jaxpr/ppermute | solution.py:19
  330.0 10.7 %collective-permute-done = f32[16,64,128]{2,1,0:T(8,128)S(1)} collective-permute-done((f32[16,64,128]{2,1,0:T(8,128)S(1)}, f32[16,64,128]{2,1,0:T(8,128)S(1)}, u32[]{:S(2)}, u32[]{:S(2)}) %collective-permute-start) | collective-permute-done | bytes 524320 | tf_op jit(solution)/shard_map/while/body/eval_jaxpr/ppermute | solution.py:19
  342.7 10.7 %collective-permute-done = f32[16,64,128]{2,1,0:T(8,128)S(1)} collective-permute-done((f32[16,64,128]{2,1,0:T(8,128)S(1)}, f32[16,64,128]{2,1,0:T(8,128)S(1)}, u32[]{:S(2)}, u32[]{:S(2)}) %collective-permute-start) | collective-permute-done | bytes 524320 | tf_op jit(solution)/shard_map/while/body/eval_jaxpr/ppermute | solution.py:19
  355.4 10.7 %collective-permute-done = f32[16,64,128]{2,1,0:T(8,128)S(1)} collective-permute-done((f32[16,64,128]{2,1,0:T(8,128)S(1)}, f32[16,64,128]{2,1,0:T(8,128)S(1)}, u32[]{:S(2)}, u32[]{:S(2)}) %collective-permute-start) | collective-permute-done | bytes 524320 | tf_op jit(solution)/shard_map/while/body/eval_jaxpr/ppermute | solution.py:19
  368.1 10.7 %collective-permute-done = f32[16,64,128]{2,1,0:T(8,128)S(1)} collective-permute-done((f32[16,64,128]{2,1,0:T(8,128)S(1)}, f32[16,64,128]{2,1,0:T(8,128)S(1)}, u32[]{:S(2)}, u32[]{:S(2)}) %collective-permute-start) | collective-permute-done | bytes 524320 | tf_op jit(solution)/shard_map/while/body/eval_jaxpr/ppermute | solution.py:19
  380.9 10.7 %collective-permute-done = f32[16,64,128]{2,1,0:T(8,128)S(1)} collective-permute-done((f32[16,64,128]{2,1,0:T(8,128)S(1)}, f32[16,64,128]{2,1,0:T(8,128)S(1)}, u32[]{:S(2)}, u32[]{:S(2)}) %collective-permute-start) | collective-permute-done | bytes 524320 | tf_op jit(solution)/shard_map/while/body/eval_jaxpr/ppermute | solution.py:19
  393.6 10.7 %collective-permute-done = f32[16,64,128]{2,1,0:T(8,128)S(1)} collective-permute-done((f32[16,64,128]{2,1,0:T(8,128)S(1)}, f32[16,64,128]{2,1,0:T(8,128)S(1)}, u32[]{:S(2)}, u32[]{:S(2)}) %collective-permute-start) | collective-permute-done | bytes 524320 | tf_op jit(solution)/shard_map/while/body/eval_jaxpr/ppermute | solution.py:19
  432.5 95.3 %reduce-scatter.2.cloned.1.call-done = f32[64,4096]{1,0:T(8,128)} async-done(((f32[512,4096]{1,0:T(8,128)}), f32[64,4096]{1,0:T(8,128)}) %reduce-scatter.2.cloned.1.call-update) | async-done | bytes 1048592 | tf_op jit(solution)/shard_map/reduce_scatter | solution.py:120
  (140 shorter events, 106.8 us)
Async XLA Ops:
  6.5 521.3 %reduce-scatter.2.cloned.1.call-start = ((), (), s32[]{:S(2)}) async-start(), calls=%async_computation.1 | async-start | bytes 9437184 | tf_op jit(solution)/shard_map/reduce_scatter | solution.py:120
  22.5 12.6 %collective-permute-start = (f32[16,64,128]{2,1,0:T(8,128)S(1)}, f32[16,64,128]{2,1,0:T(8,128)S(1)}, u32[]{:S(2)}, u32[]{:S(2)}) collective-permute-start(f32[16,64,128]{2,1,0:T(8,128)S(1)} %multiply_add_fusion.2), channel_id=1, source_target_pairs={{0,8},{8,16},{16,24},{24,32},{32,40},{40,48},{48,56},{56,64},{64,7... | collective-permute-start | bytes 1572872 | tf_op jit(solution)/shard_map/while/body/eval_jaxpr/ppermute | solution.py:19
  35.2 12.6 %collective-permute-start = (f32[16,64,128]{2,1,0:T(8,128)S(1)}, f32[16,64,128]{2,1,0:T(8,128)S(1)}, u32[]{:S(2)}, u32[]{:S(2)}) collective-permute-start(f32[16,64,128]{2,1,0:T(8,128)S(1)} %multiply_add_fusion.2), channel_id=1, source_target_pairs={{0,8},{8,16},{16,24},{24,32},{32,40},{40,48},{48,56},{56,64},{64,7... | collective-permute-start | bytes 1572872 | tf_op jit(solution)/shard_map/while/body/eval_jaxpr/ppermute | solution.py:19
  48.0 12.6 %collective-permute-start = (f32[16,64,128]{2,1,0:T(8,128)S(1)}, f32[16,64,128]{2,1,0:T(8,128)S(1)}, u32[]{:S(2)}, u32[]{:S(2)}) collective-permute-start(f32[16,64,128]{2,1,0:T(8,128)S(1)} %multiply_add_fusion.2), channel_id=1, source_target_pairs={{0,8},{8,16},{16,24},{24,32},{32,40},{40,48},{48,56},{56,64},{64,7... | collective-permute-start | bytes 1572872 | tf_op jit(solution)/shard_map/while/body/eval_jaxpr/ppermute | solution.py:19
  60.7 12.6 %collective-permute-start = (f32[16,64,128]{2,1,0:T(8,128)S(1)}, f32[16,64,128]{2,1,0:T(8,128)S(1)}, u32[]{:S(2)}, u32[]{:S(2)}) collective-permute-start(f32[16,64,128]{2,1,0:T(8,128)S(1)} %multiply_add_fusion.2), channel_id=1, source_target_pairs={{0,8},{8,16},{16,24},{24,32},{32,40},{40,48},{48,56},{56,64},{64,7... | collective-permute-start | bytes 1572872 | tf_op jit(solution)/shard_map/while/body/eval_jaxpr/ppermute | solution.py:19
  73.4 12.6 %collective-permute-start = (f32[16,64,128]{2,1,0:T(8,128)S(1)}, f32[16,64,128]{2,1,0:T(8,128)S(1)}, u32[]{:S(2)}, u32[]{:S(2)}) collective-permute-start(f32[16,64,128]{2,1,0:T(8,128)S(1)} %multiply_add_fusion.2), channel_id=1, source_target_pairs={{0,8},{8,16},{16,24},{24,32},{32,40},{40,48},{48,56},{56,64},{64,7... | collective-permute-start | bytes 1572872 | tf_op jit(solution)/shard_map/while/body/eval_jaxpr/ppermute | solution.py:19
  86.2 12.6 %collective-permute-start = (f32[16,64,128]{2,1,0:T(8,128)S(1)}, f32[16,64,128]{2,1,0:T(8,128)S(1)}, u32[]{:S(2)}, u32[]{:S(2)}) collective-permute-start(f32[16,64,128]{2,1,0:T(8,128)S(1)} %multiply_add_fusion.2), channel_id=1, source_target_pairs={{0,8},{8,16},{16,24},{24,32},{32,40},{40,48},{48,56},{56,64},{64,7... | collective-permute-start | bytes 1572872 | tf_op jit(solution)/shard_map/while/body/eval_jaxpr/ppermute | solution.py:19
  98.9 12.6 %collective-permute-start = (f32[16,64,128]{2,1,0:T(8,128)S(1)}, f32[16,64,128]{2,1,0:T(8,128)S(1)}, u32[]{:S(2)}, u32[]{:S(2)}) collective-permute-start(f32[16,64,128]{2,1,0:T(8,128)S(1)} %multiply_add_fusion.2), channel_id=1, source_target_pairs={{0,8},{8,16},{16,24},{24,32},{32,40},{40,48},{48,56},{56,64},{64,7... | collective-permute-start | bytes 1572872 | tf_op jit(solution)/shard_map/while/body/eval_jaxpr/ppermute | solution.py:19
  111.6 12.6 %collective-permute-start = (f32[16,64,128]{2,1,0:T(8,128)S(1)}, f32[16,64,128]{2,1,0:T(8,128)S(1)}, u32[]{:S(2)}, u32[]{:S(2)}) collective-permute-start(f32[16,64,128]{2,1,0:T(8,128)S(1)} %multiply_add_fusion.2), channel_id=1, source_target_pairs={{0,8},{8,16},{16,24},{24,32},{32,40},{40,48},{48,56},{56,64},{64,7... | collective-permute-start | bytes 1572872 | tf_op jit(solution)/shard_map/while/body/eval_jaxpr/ppermute | solution.py:19
  124.3 12.6 %collective-permute-start = (f32[16,64,128]{2,1,0:T(8,128)S(1)}, f32[16,64,128]{2,1,0:T(8,128)S(1)}, u32[]{:S(2)}, u32[]{:S(2)}) collective-permute-start(f32[16,64,128]{2,1,0:T(8,128)S(1)} %multiply_add_fusion.2), channel_id=1, source_target_pairs={{0,8},{8,16},{16,24},{24,32},{32,40},{40,48},{48,56},{56,64},{64,7... | collective-permute-start | bytes 1572872 | tf_op jit(solution)/shard_map/while/body/eval_jaxpr/ppermute | solution.py:19
  137.1 12.6 %collective-permute-start = (f32[16,64,128]{2,1,0:T(8,128)S(1)}, f32[16,64,128]{2,1,0:T(8,128)S(1)}, u32[]{:S(2)}, u32[]{:S(2)}) collective-permute-start(f32[16,64,128]{2,1,0:T(8,128)S(1)} %multiply_add_fusion.2), channel_id=1, source_target_pairs={{0,8},{8,16},{16,24},{24,32},{32,40},{40,48},{48,56},{56,64},{64,7... | collective-permute-start | bytes 1572872 | tf_op jit(solution)/shard_map/while/body/eval_jaxpr/ppermute | solution.py:19
  149.8 12.6 %collective-permute-start = (f32[16,64,128]{2,1,0:T(8,128)S(1)}, f32[16,64,128]{2,1,0:T(8,128)S(1)}, u32[]{:S(2)}, u32[]{:S(2)}) collective-permute-start(f32[16,64,128]{2,1,0:T(8,128)S(1)} %multiply_add_fusion.2), channel_id=1, source_target_pairs={{0,8},{8,16},{16,24},{24,32},{32,40},{40,48},{48,56},{56,64},{64,7... | collective-permute-start | bytes 1572872 | tf_op jit(solution)/shard_map/while/body/eval_jaxpr/ppermute | solution.py:19
  162.5 12.6 %collective-permute-start = (f32[16,64,128]{2,1,0:T(8,128)S(1)}, f32[16,64,128]{2,1,0:T(8,128)S(1)}, u32[]{:S(2)}, u32[]{:S(2)}) collective-permute-start(f32[16,64,128]{2,1,0:T(8,128)S(1)} %multiply_add_fusion.2), channel_id=1, source_target_pairs={{0,8},{8,16},{16,24},{24,32},{32,40},{40,48},{48,56},{56,64},{64,7... | collective-permute-start | bytes 1572872 | tf_op jit(solution)/shard_map/while/body/eval_jaxpr/ppermute | solution.py:19
  175.3 12.6 %collective-permute-start = (f32[16,64,128]{2,1,0:T(8,128)S(1)}, f32[16,64,128]{2,1,0:T(8,128)S(1)}, u32[]{:S(2)}, u32[]{:S(2)}) collective-permute-start(f32[16,64,128]{2,1,0:T(8,128)S(1)} %multiply_add_fusion.2), channel_id=1, source_target_pairs={{0,8},{8,16},{16,24},{24,32},{32,40},{40,48},{48,56},{56,64},{64,7... | collective-permute-start | bytes 1572872 | tf_op jit(solution)/shard_map/while/body/eval_jaxpr/ppermute | solution.py:19
  188.0 12.6 %collective-permute-start = (f32[16,64,128]{2,1,0:T(8,128)S(1)}, f32[16,64,128]{2,1,0:T(8,128)S(1)}, u32[]{:S(2)}, u32[]{:S(2)}) collective-permute-start(f32[16,64,128]{2,1,0:T(8,128)S(1)} %multiply_add_fusion.2), channel_id=1, source_target_pairs={{0,8},{8,16},{16,24},{24,32},{32,40},{40,48},{48,56},{56,64},{64,7... | collective-permute-start | bytes 1572872 | tf_op jit(solution)/shard_map/while/body/eval_jaxpr/ppermute | solution.py:19
  200.7 12.6 %collective-permute-start = (f32[16,64,128]{2,1,0:T(8,128)S(1)}, f32[16,64,128]{2,1,0:T(8,128)S(1)}, u32[]{:S(2)}, u32[]{:S(2)}) collective-permute-start(f32[16,64,128]{2,1,0:T(8,128)S(1)} %multiply_add_fusion.2), channel_id=1, source_target_pairs={{0,8},{8,16},{16,24},{24,32},{32,40},{40,48},{48,56},{56,64},{64,7... | collective-permute-start | bytes 1572872 | tf_op jit(solution)/shard_map/while/body/eval_jaxpr/ppermute | solution.py:19
  213.5 12.6 %collective-permute-start = (f32[16,64,128]{2,1,0:T(8,128)S(1)}, f32[16,64,128]{2,1,0:T(8,128)S(1)}, u32[]{:S(2)}, u32[]{:S(2)}) collective-permute-start(f32[16,64,128]{2,1,0:T(8,128)S(1)} %multiply_add_fusion.2), channel_id=1, source_target_pairs={{0,8},{8,16},{16,24},{24,32},{32,40},{40,48},{48,56},{56,64},{64,7... | collective-permute-start | bytes 1572872 | tf_op jit(solution)/shard_map/while/body/eval_jaxpr/ppermute | solution.py:19
  226.2 12.6 %collective-permute-start = (f32[16,64,128]{2,1,0:T(8,128)S(1)}, f32[16,64,128]{2,1,0:T(8,128)S(1)}, u32[]{:S(2)}, u32[]{:S(2)}) collective-permute-start(f32[16,64,128]{2,1,0:T(8,128)S(1)} %multiply_add_fusion.2), channel_id=1, source_target_pairs={{0,8},{8,16},{16,24},{24,32},{32,40},{40,48},{48,56},{56,64},{64,7... | collective-permute-start | bytes 1572872 | tf_op jit(solution)/shard_map/while/body/eval_jaxpr/ppermute | solution.py:19
  238.9 12.6 %collective-permute-start = (f32[16,64,128]{2,1,0:T(8,128)S(1)}, f32[16,64,128]{2,1,0:T(8,128)S(1)}, u32[]{:S(2)}, u32[]{:S(2)}) collective-permute-start(f32[16,64,128]{2,1,0:T(8,128)S(1)} %multiply_add_fusion.2), channel_id=1, source_target_pairs={{0,8},{8,16},{16,24},{24,32},{32,40},{40,48},{48,56},{56,64},{64,7... | collective-permute-start | bytes 1572872 | tf_op jit(solution)/shard_map/while/body/eval_jaxpr/ppermute | solution.py:19
  251.6 12.6 %collective-permute-start = (f32[16,64,128]{2,1,0:T(8,128)S(1)}, f32[16,64,128]{2,1,0:T(8,128)S(1)}, u32[]{:S(2)}, u32[]{:S(2)}) collective-permute-start(f32[16,64,128]{2,1,0:T(8,128)S(1)} %multiply_add_fusion.2), channel_id=1, source_target_pairs={{0,8},{8,16},{16,24},{24,32},{32,40},{40,48},{48,56},{56,64},{64,7... | collective-permute-start | bytes 1572872 | tf_op jit(solution)/shard_map/while/body/eval_jaxpr/ppermute | solution.py:19
  264.4 12.6 %collective-permute-start = (f32[16,64,128]{2,1,0:T(8,128)S(1)}, f32[16,64,128]{2,1,0:T(8,128)S(1)}, u32[]{:S(2)}, u32[]{:S(2)}) collective-permute-start(f32[16,64,128]{2,1,0:T(8,128)S(1)} %multiply_add_fusion.2), channel_id=1, source_target_pairs={{0,8},{8,16},{16,24},{24,32},{32,40},{40,48},{48,56},{56,64},{64,7... | collective-permute-start | bytes 1572872 | tf_op jit(solution)/shard_map/while/body/eval_jaxpr/ppermute | solution.py:19
  277.1 12.6 %collective-permute-start = (f32[16,64,128]{2,1,0:T(8,128)S(1)}, f32[16,64,128]{2,1,0:T(8,128)S(1)}, u32[]{:S(2)}, u32[]{:S(2)}) collective-permute-start(f32[16,64,128]{2,1,0:T(8,128)S(1)} %multiply_add_fusion.2), channel_id=1, source_target_pairs={{0,8},{8,16},{16,24},{24,32},{32,40},{40,48},{48,56},{56,64},{64,7... | collective-permute-start | bytes 1572872 | tf_op jit(solution)/shard_map/while/body/eval_jaxpr/ppermute | solution.py:19
  289.8 12.6 %collective-permute-start = (f32[16,64,128]{2,1,0:T(8,128)S(1)}, f32[16,64,128]{2,1,0:T(8,128)S(1)}, u32[]{:S(2)}, u32[]{:S(2)}) collective-permute-start(f32[16,64,128]{2,1,0:T(8,128)S(1)} %multiply_add_fusion.2), channel_id=1, source_target_pairs={{0,8},{8,16},{16,24},{24,32},{32,40},{40,48},{48,56},{56,64},{64,7... | collective-permute-start | bytes 1572872 | tf_op jit(solution)/shard_map/while/body/eval_jaxpr/ppermute | solution.py:19
  302.6 12.6 %collective-permute-start = (f32[16,64,128]{2,1,0:T(8,128)S(1)}, f32[16,64,128]{2,1,0:T(8,128)S(1)}, u32[]{:S(2)}, u32[]{:S(2)}) collective-permute-start(f32[16,64,128]{2,1,0:T(8,128)S(1)} %multiply_add_fusion.2), channel_id=1, source_target_pairs={{0,8},{8,16},{16,24},{24,32},{32,40},{40,48},{48,56},{56,64},{64,7... | collective-permute-start | bytes 1572872 | tf_op jit(solution)/shard_map/while/body/eval_jaxpr/ppermute | solution.py:19
  315.3 12.6 %collective-permute-start = (f32[16,64,128]{2,1,0:T(8,128)S(1)}, f32[16,64,128]{2,1,0:T(8,128)S(1)}, u32[]{:S(2)}, u32[]{:S(2)}) collective-permute-start(f32[16,64,128]{2,1,0:T(8,128)S(1)} %multiply_add_fusion.2), channel_id=1, source_target_pairs={{0,8},{8,16},{16,24},{24,32},{32,40},{40,48},{48,56},{56,64},{64,7... | collective-permute-start | bytes 1572872 | tf_op jit(solution)/shard_map/while/body/eval_jaxpr/ppermute | solution.py:19
  328.0 12.6 %collective-permute-start = (f32[16,64,128]{2,1,0:T(8,128)S(1)}, f32[16,64,128]{2,1,0:T(8,128)S(1)}, u32[]{:S(2)}, u32[]{:S(2)}) collective-permute-start(f32[16,64,128]{2,1,0:T(8,128)S(1)} %multiply_add_fusion.2), channel_id=1, source_target_pairs={{0,8},{8,16},{16,24},{24,32},{32,40},{40,48},{48,56},{56,64},{64,7... | collective-permute-start | bytes 1572872 | tf_op jit(solution)/shard_map/while/body/eval_jaxpr/ppermute | solution.py:19
  340.8 12.6 %collective-permute-start = (f32[16,64,128]{2,1,0:T(8,128)S(1)}, f32[16,64,128]{2,1,0:T(8,128)S(1)}, u32[]{:S(2)}, u32[]{:S(2)}) collective-permute-start(f32[16,64,128]{2,1,0:T(8,128)S(1)} %multiply_add_fusion.2), channel_id=1, source_target_pairs={{0,8},{8,16},{16,24},{24,32},{32,40},{40,48},{48,56},{56,64},{64,7... | collective-permute-start | bytes 1572872 | tf_op jit(solution)/shard_map/while/body/eval_jaxpr/ppermute | solution.py:19
  353.5 12.6 %collective-permute-start = (f32[16,64,128]{2,1,0:T(8,128)S(1)}, f32[16,64,128]{2,1,0:T(8,128)S(1)}, u32[]{:S(2)}, u32[]{:S(2)}) collective-permute-start(f32[16,64,128]{2,1,0:T(8,128)S(1)} %multiply_add_fusion.2), channel_id=1, source_target_pairs={{0,8},{8,16},{16,24},{24,32},{32,40},{40,48},{48,56},{56,64},{64,7... | collective-permute-start | bytes 1572872 | tf_op jit(solution)/shard_map/while/body/eval_jaxpr/ppermute | solution.py:19
  366.2 12.6 %collective-permute-start = (f32[16,64,128]{2,1,0:T(8,128)S(1)}, f32[16,64,128]{2,1,0:T(8,128)S(1)}, u32[]{:S(2)}, u32[]{:S(2)}) collective-permute-start(f32[16,64,128]{2,1,0:T(8,128)S(1)} %multiply_add_fusion.2), channel_id=1, source_target_pairs={{0,8},{8,16},{16,24},{24,32},{32,40},{40,48},{48,56},{56,64},{64,7... | collective-permute-start | bytes 1572872 | tf_op jit(solution)/shard_map/while/body/eval_jaxpr/ppermute | solution.py:19
  378.9 12.6 %collective-permute-start = (f32[16,64,128]{2,1,0:T(8,128)S(1)}, f32[16,64,128]{2,1,0:T(8,128)S(1)}, u32[]{:S(2)}, u32[]{:S(2)}) collective-permute-start(f32[16,64,128]{2,1,0:T(8,128)S(1)} %multiply_add_fusion.2), channel_id=1, source_target_pairs={{0,8},{8,16},{16,24},{24,32},{32,40},{40,48},{48,56},{56,64},{64,7... | collective-permute-start | bytes 1572872 | tf_op jit(solution)/shard_map/while/body/eval_jaxpr/ppermute | solution.py:19
  391.7 12.6 %collective-permute-start = (f32[16,64,128]{2,1,0:T(8,128)S(1)}, f32[16,64,128]{2,1,0:T(8,128)S(1)}, u32[]{:S(2)}, u32[]{:S(2)}) collective-permute-start(f32[16,64,128]{2,1,0:T(8,128)S(1)} %multiply_add_fusion.2), channel_id=1, source_target_pairs={{0,8},{8,16},{16,24},{24,32},{32,40},{40,48},{48,56},{56,64},{64,7... | collective-permute-start | bytes 1572872 | tf_op jit(solution)/shard_map/while/body/eval_jaxpr/ppermute | solution.py:19
  404.4 12.6 %collective-permute-start = (f32[16,64,128]{2,1,0:T(8,128)S(1)}, f32[16,64,128]{2,1,0:T(8,128)S(1)}, u32[]{:S(2)}, u32[]{:S(2)}) collective-permute-start(f32[16,64,128]{2,1,0:T(8,128)S(1)} %multiply_add_fusion.2), channel_id=1, source_target_pairs={{0,8},{8,16},{16,24},{24,32},{32,40},{40,48},{48,56},{56,64},{64,7... | collective-permute-start | bytes 1572872 | tf_op jit(solution)/shard_map/while/body/eval_jaxpr/ppermute | solution.py:19
  (16 other events, 453.1 us)
Sparse Core Ops, SparseCore 0:
  432.6 95.1 reduce-scatter.1
where the time goes:
time: 539 us; the launch traced here: 537 us
  waiting for transfers between devices  426 us (79%)
  starting transfers between devices  59.5 us (11%)
  between operations  13.6 us (3%)
  other arithmetic  12.4 us (2%)
  matrix products  12.4 us (2%)
  local copies, waits for them, and re-layouts  11.8 us (2%)
    ppermute x31, waiting for transfers between devices, passed_along(): lax.ppermute(value, axis, [(source, source + steps) for source in range(i...  331 us
    reduce_scatter x1, waiting for transfers between devices, body(): lax.psum_scatter(jnp.dot(normed, out_weight, preferred_element_type=jnp.f...  95.3 us
    ppermute x31, starting transfers between devices, passed_along(): lax.ppermute(value, axis, [(source, source + steps) for source in range(i...  59.5 us
  transfers between devices with their start and end apart: 32, of which 32 were waited for; matrix products, arithmetic and copies ran while one was open for 0% of the time, Pallas kernels for 0%

commit v1 on v0

v1 whole, which is shorter than its diff:
```python
import functools

import jax
import jax.numpy as jnp
from jax import lax
from jax.experimental import pallas as pl
from jax.experimental.pallas import tpu as pltpu
from jax.sharding import PartitionSpec as P

MESH = pl.DeviceIdType.MESH
F32 = jnp.float32
BF16 = jnp.bfloat16

HEAD_DIM = 64
NSTATE = 128
SPAN = 256
EPS = 1e-05
MASKED = -1e30
PIECES = 4
EARLY = (4, 4)


def split3(value):
    high = value.astype(BF16)
    rest = value - high.astype(F32)
    mid = rest.astype(BF16)
    low = (rest - mid.astype(F32)).astype(BF16)
    return high, mid, low


def kernel(
    n_ctx,
    n_head,
    feat_hbm,
    gate_hbm,
    write_hbm,
    read_hbm,
    step_hbm,
    decay_hbm,
    starts_hbm,
    skip_hbm,
    gain_hbm,
    weight_hbm,
    out_ref,
    feat,
    gate,
    write,
    read,
    step,
    decay,
    starts,
    skip,
    gain,
    weight,
    write_t,
    rows_u,
    rows_seg,
    cols,
    expand,
    skip_row,
    ready,
    reach,
    state0,
    keep0,
    total,
    partner_part,
    first_state,
    send1,
    recv1,
    send2,
    recv2,
    send3,
    recv3,
    entry,
    normed,
    ring,
    in_sem,
    pair_send,
    pair_recv,
    ex_send,
    ex_recv,
    ring_send,
    ring_recv,
):
    ctx = lax.axis_index("ctx")
    z = lax.axis_index("head")
    core = lax.rem(ctx, 2)
    chip = ctx // 2
    chips = n_ctx // 2
    other = ctx + 1 - 2 * core
    heads = step.shape[0]
    blocks, span, chans = feat.shape
    half = chans // 2
    chunk = blocks * span // n_head
    per_block = span // chunk
    width = ring.shape[3]
    target = lax.rem(z + 1 + (n_head - 2) * core, n_head)

    barrier = pltpu.get_barrier_semaphore()
    pl.semaphore_signal(barrier, inc=1, device_id={"ctx": other, "head": z}, device_id_type=MESH)
    for offset in (1, n_head - 1):
        pl.semaphore_signal(
            barrier, inc=1, device_id={"ctx": ctx, "head": lax.rem(z + offset, n_head)}, device_id_type=MESH
        )

    def greet(offset, carry):
        peer = 2 * lax.rem(chip + offset, chips) + core
        pl.semaphore_signal(barrier, inc=1, device_id={"ctx": peer, "head": z}, device_id_type=MESH)
        return carry

    lax.fori_loop(1, chips, greet, 0)

    loads = {}
    for index, (name, source, dest) in enumerate(
        [
            ("decay", decay_hbm, decay),
            ("starts", starts_hbm, starts),
            ("step", step_hbm, step),
            ("write", write_hbm, write),
            ("feat", feat_hbm, feat),
            ("read", read_hbm, read),
            ("gate", gate_hbm, gate),
            ("skip", skip_hbm, skip),
            ("gain", gain_hbm, gain),
            ("weight", weight_hbm, weight),
        ]
    ):
        loads[name] = pltpu.make_async_copy(source, dest, in_sem.at[index])
        loads[name].start()

    row_id = lax.broadcasted_iota(jnp.int32, (span, span), 0)
    col_id = lax.broadcasted_iota(jnp.int32, (span, span), 1)
    upto = (row_id <= col_id).astype(F32).astype(BF16)
    head_of = lax.broadcasted_iota(jnp.int32, (heads, chans), 1) // HEAD_DIM
    pick = (head_of == lax.broadcasted_iota(jnp.int32, (heads, chans), 0)).astype(F32)

    def spread(column):
        return jnp.sum(column * pick, axis=0, keepdims=True)

    lane_head = lax.broadcasted_iota(jnp.int32, (1, 256), 1) // HEAD_DIM

    def diagonal(stacked, rows):
        result = stacked[0:rows]
        for i in range(1, 4):
            result = jnp.where(lane_head == i, stacked[i * rows : (i + 1) * rows], result)
        return result

    loads["decay"].wait()
    loads["starts"].wait()
    sums = []
    for k in range(blocks):
        tokens = slice(k * span, (k + 1) * span)
        start_rows = jnp.broadcast_to(starts[:, tokens].astype(F32), (heads, span)).astype(BF16)
        stacked = jnp.concatenate([*split3(decay[:, tokens]), start_rows], axis=0)
        sums.append(jnp.dot(stacked, upto, preferred_element_type=F32))
    loads["step"].wait()
    loads["write"].wait()
    keeps, states, tails, cums, segs = [], [], [], [], []
    for k in range(blocks):
        tokens = slice(k * span, (k + 1) * span)
        cum = sums[k][0:heads] + sums[k][heads : 2 * heads] + sums[k][2 * heads : 3 * heads]
        seg = sums[k][3 * heads : 3 * heads + 1]
        last = cum[:, span - 1 : span]
        seg_last = seg[:, span - 1 : span]
        tails.append(jnp.where(seg == seg_last, jnp.exp(last - cum), 0.0) * step[:, tokens])
        keeps.append(spread(jnp.where(seg_last == 0.0, jnp.exp(last), 0.0)))
        cums.append(cum)
        segs.append(seg)
    loads["feat"].wait()
    for k in range(blocks):
        turned = jnp.transpose(write[k].astype(F32))
        write_t[k] = turned.astype(BF16)
        parts = []
        for quad in range(heads // 4):
            lhs = jnp.concatenate(
                [(turned * tails[k][4 * quad + i : 4 * quad + i + 1]).astype(BF16) for i in range(4)], axis=0
            )
            full = jnp.dot(lhs, feat[k, :, 256 * quad : 256 * (quad + 1)], preferred_element_type=F32)
            parts.append(diagonal(full, NSTATE))
        states.append(parts)
    per_half = half // 256
    for h in range(2):
        cut = slice(h * half, (h + 1) * half)
        keep0[h] = jnp.broadcast_to(keeps[0][:, cut], (8, half))
        total[h, NSTATE:] = jnp.broadcast_to((keeps[0] * keeps[1])[:, cut], (8, half))
        for part in range(per_half):
            lanes = slice(256 * part, 256 * (part + 1))
            chans_at = slice(h * half + 256 * part, h * half + 256 * (part + 1))
            first = states[0][h * per_half + part]
            state0[h, :, lanes] = first
            total[h, :NSTATE, lanes] = keeps[1][:, chans_at] * first + states[1][h * per_half + part]

    pl.semaphore_wait(barrier, chips + 2)
    pair1 = pltpu.make_async_remote_copy(
        src_ref=total.at[1 - core],
        dst_ref=partner_part,
        send_sem=pair_send.at[0],
        recv_sem=pair_recv.at[0],
        device_id={"ctx": other, "head": z},
        device_id_type=MESH,
    )
    pair1.start()

    def columns_of_block(k):
        tokens = slice(k * span, (k + 1) * span)
        rows_u[k] = cums[k] - jnp.log(step[:, tokens])
        rows_seg[k] = jnp.broadcast_to(segs[k], (8, span))
        reach_scale = jnp.where(segs[k] == 0.0, jnp.exp(cums[k]), 0.0)
        pieces = [part.astype(F32) for part in split3(reach_scale)]
        seg_rows = jnp.broadcast_to(segs[k], (heads, span))
        pad = jnp.zeros((NSTATE - 5 * heads, span), F32)
        cols[tokens] = jnp.transpose(jnp.concatenate([cums[k], *pieces, seg_rows, pad], axis=0))

    for k in range(blocks):
        columns_of_block(k)
    line = lax.broadcasted_iota(jnp.int32, (NSTATE, chans), 0)
    owner = lax.broadcasted_iota(jnp.int32, (NSTATE, chans), 1) // HEAD_DIM
    inside = (line >= heads) & (line < 4 * heads)
    expand[...] = jnp.where(inside & (lax.rem(line, heads) == owner), 1.0, 0.0).astype(BF16)
    loads["skip"].wait()
    square = jnp.broadcast_to(skip[...], (heads, heads))
    same = lax.broadcasted_iota(jnp.int32, (heads, heads), 0) == lax.broadcasted_iota(jnp.int32, (heads, heads), 1)
    skip_row[...] = spread(jnp.sum(jnp.where(same, square, 0.0), axis=1, keepdims=True))
    ring[0] = jnp.zeros_like(ring[0])

    pair1.wait_recv()
    mine = total[core]
    theirs = partner_part[...]
    leads = core == 0
    s0 = jnp.where(leads, mine[:NSTATE], theirs[:NSTATE])
    s1 = jnp.where(leads, theirs[:NSTATE], mine[:NSTATE])
    m0 = jnp.where(leads, mine[NSTATE:], theirs[NSTATE:])
    m1 = jnp.where(leads, theirs[NSTATE:], mine[NSTATE:])
    first_state[:NSTATE] = s0
    first_state[NSTATE:] = m0
    joined = m1[0:1] * s0 + s1
    joined_mult = m0 * m1
    across = half // 128
    deep = NSTATE // (chips // across)
    for q in range(chips):
        rows = slice(deep * (q // across), deep * (q // across + 1))
        lanes = slice(128 * (q % across), 128 * (q % across + 1))
        send1[q, :deep] = joined[rows, lanes]
        send1[q, deep:] = joined_mult[:, lanes]

    def exchange1(offset):
        peer = lax.rem(chip + offset, chips)
        return pltpu.make_async_remote_copy(
            src_ref=send1.at[peer],
            dst_ref=recv1.at[chip],
            send_sem=ex_send.at[0, peer],
            recv_sem=ex_recv.at[0, chip],
            device_id={"ctx": 2 * peer + core, "head": z},
            device_id_type=MESH,
        )

    def start1(offset, carry):
        exchange1(offset).start()
        return carry

    lax.fori_loop(1, chips, start1, 0)
    recv1[chip] = send1[chip]

    def chunk_of(s):
        return lax.rem(z + (1 - core) * (n_head - 1 - s) + core * (1 + s), n_head)

    loads["read"].wait()
    loads["gate"].wait()
    loads["gain"].wait()

    def prepare(s):
        b = chunk_of(s)
        k = b // per_block
        local = pl.multiple_of(lax.rem(b, per_block) * chunk, chunk)
        at = pl.multiple_of(b * chunk, chunk)
        scores = jnp.dot(read[k, pl.ds(local, chunk), :], write_t[k], preferred_element_type=F32)
        column = cols[pl.ds(at, chunk), :]
        seg_row = rows_seg[k][0:1]
        seg_col = column[:, 4 * heads : 4 * heads + 1]
        later = local + lax.broadcasted_iota(jnp.int32, (chunk, span), 0)
        earlier = lax.broadcasted_iota(jnp.int32, (chunk, span), 1)
        mask = jnp.where((seg_col == seg_row) & (earlier <= later), 0.0, MASKED)
        u = rows_u[k]
        scale = jnp.dot(column.astype(BF16), expand[...], preferred_element_type=F32)
        for quad in range(heads // 4):
            lanes = slice(256 * quad, 256 * (quad + 1))
            stack = []
            for h in range(4 * quad, 4 * quad + 4):
                spread_log = column[:, h : h + 1] - u[h : h + 1] + mask
                stack.append((jnp.exp(spread_log) * scores).astype(BF16))
            full = jnp.dot(jnp.concatenate(stack, axis=0), feat[k, :, lanes], preferred_element_type=F32)
            gates = gate[k, pl.ds(local, chunk), lanes].astype(F32)
            silu = gates * jax.nn.sigmoid(gates)
            direct = skip_row[:, lanes] * feat[k, pl.ds(local, chunk), lanes].astype(F32)
            ready[s, :, lanes] = (diagonal(full, chunk) + direct) * silu
            reach[s, :, lanes] = scale[:, lanes] * silu

    def prepare_loop(low, high):
        def run(s, carry):
            prepare(s)
            return carry

        lax.fori_loop(low, high, run, 0)

    prepare_loop(0, EARLY[0])

    def back(peer):
        return pltpu.make_async_remote_copy(
            src_ref=send2.at[peer],
            dst_ref=recv2.at[chip],
            send_sem=ex_send.at[1, peer],
            recv_sem=ex_recv.at[1, chip],
            device_id={"ctx": 2 * peer + core, "head": z},
            device_id_type=MESH,
        )

    def arrival(round_, peer, dest):
        return pltpu.make_async_remote_copy(
            src_ref=dest.at[peer],
            dst_ref=dest.at[peer],
            send_sem=ex_send.at[round_, peer],
            recv_sem=ex_recv.at[round_, peer],
            device_id={"ctx": 2 * peer + core, "head": z},
            device_id_type=MESH,
        )

    def scan_step(p, state):
        send2[p] = state

        @pl.when(p != chip)
        def _():
            back(p).start()
            arrival(0, p, recv1).wait_recv()

        return recv1[p, deep : deep + 1] * state + recv1[p, :deep]

    lax.fori_loop(0, chips, scan_step, jnp.zeros((deep, 128), F32))
    recv2[chip] = send2[chip]

    prepare_loop(EARLY[0], EARLY[0] + EARLY[1])

    def await2(offset, carry):
        arrival(1, lax.rem(chip + offset, chips), recv2).wait_recv()
        return carry

    lax.fori_loop(1, chips, await2, 0)
    strips = []
    for down in range(chips // across):
        strips.append(jnp.concatenate([recv2[down * across + right] for right in range(across)], axis=1))
    entry0 = jnp.concatenate(strips, axis=0)
    entry1 = first_state[NSTATE : NSTATE + 1] * entry0 + first_state[:NSTATE]
    send3[...] = jnp.where(leads, entry1, entry0)
    pair2 = pltpu.make_async_remote_copy(
        src_ref=send3,
        dst_ref=recv3,
        send_sem=pair_send.at[1],
        recv_sem=pair_recv.at[1],
        device_id={"ctx": other, "head": z},
        device_id_type=MESH,
    )
    pair2.start()

    def set_entry(h, value):
        entry[0, h] = value.astype(BF16)
        entry[1, h] = (keep0[h][0:1] * value + state0[h]).astype(BF16)

    set_entry(core, jnp.where(leads, entry0, entry1))
    loads["weight"].wait()
    pair2.wait_recv()
    set_entry(1 - core, recv3[...])

    def hop(s, piece):
        return pltpu.make_async_remote_copy(
            src_ref=ring.at[s, piece],
            dst_ref=ring.at[s + 1, piece],
            send_sem=ring_send.at[s, piece],
            recv_sem=ring_recv.at[s, piece],
            device_id={"ctx": ctx, "head": target},
            device_id_type=MESH,
        )

    def ring_step(s, carry):
        b = chunk_of(s)
        k = b // per_block
        local = pl.multiple_of(lax.rem(b, per_block) * chunk, chunk)
        reads = read[k, pl.ds(local, chunk), :]
        gated = []
        squares = jnp.zeros((chunk, 1), F32)
        for h in range(2):
            lanes = slice(h * half, (h + 1) * half)
            carried = jnp.dot(reads, entry[k, h], preferred_element_type=F32)
            value = ready[s, :, lanes] + reach[s, :, lanes] * carried
            squares = squares + jnp.sum(value * value, axis=1, keepdims=True)
            gated.append(value)
        scale = lax.rsqrt(squares * (1.0 / chans) + EPS)
        for h in range(2):
            lanes = slice(h * half, (h + 1) * half)
            normed[:, lanes] = (gated[h] * scale * gain[:, lanes]).astype(BF16)
        for piece in range(PIECES):
            lanes = slice(piece * width, (piece + 1) * width)
            own = jnp.dot(normed[...], weight[:, lanes], preferred_element_type=F32)

            @pl.when(s > 0)
            def _():
                hop(s - 1, piece).wait_recv()

            ring[s, piece] = ring[s, piece] + own

            @pl.when(s < n_head - 1)
            def _():
                hop(s, piece).start()


        return carry

    lax.fori_loop(0, n_head, ring_step, 0)
    for piece in range(PIECES):
        out_ref[:, piece * width : (piece + 1) * width] = ring[n_head - 1, piece].astype(BF16)

    pair1.wait_send()
    pair2.wait_send()

    def drain(offset, carry):
        peer = lax.rem(chip + offset, chips)
        arrival(0, peer, recv1).wait_send()
        arrival(1, peer, recv2).wait_send()
        return carry

    lax.fori_loop(1, chips, drain, 0)

    def drain_ring(s, carry):
        for piece in range(PIECES):
            hop(s, piece).wait_send()
        return carry

    lax.fori_loop(0, n_head - 1, drain_ring, 0)


def solution(mesh):
    n_ctx, n_head = mesh.shape["ctx"], mesh.shape["head"]

    def body(features, gate_values, write_proj, read_proj, step_size, log_decay, starts, skip_weight, norm_gain, out_weight):
        tokens, chans = features.shape
        heads = step_size.shape[0]
        blocks = tokens // SPAN
        width_out = out_weight.shape[1]
        chunk = tokens // n_head
        half = chans // 2
        chips = n_ctx // 2
        across = half // 128
        deep = NSTATE // (chips // across)
        width = width_out // PIECES
        dma = pltpu.SemaphoreType.DMA
        scratch = [
            pltpu.VMEM((blocks, SPAN, chans), BF16),
            pltpu.VMEM((blocks, SPAN, chans), BF16),
            pltpu.VMEM((blocks, SPAN, NSTATE), BF16),
            pltpu.VMEM((blocks, SPAN, NSTATE), BF16),
            pltpu.VMEM((heads, tokens), F32),
            pltpu.VMEM((heads, tokens), F32),
            pltpu.VMEM((1, tokens), jnp.int32),
            pltpu.VMEM((1, heads), F32),
            pltpu.VMEM((1, chans), F32),
            pltpu.VMEM((chans, width_out), BF16),
            pltpu.VMEM((blocks, NSTATE, SPAN), BF16),
            pltpu.VMEM((blocks, heads, SPAN), F32),
            pltpu.VMEM((blocks, 8, SPAN), F32),
            pltpu.VMEM((tokens, NSTATE), F32),
            pltpu.VMEM((NSTATE, chans), BF16),
            pltpu.VMEM((1, chans), F32),
            pltpu.VMEM((n_head, chunk, chans), F32),
            pltpu.VMEM((n_head, chunk, chans), F32),
            pltpu.VMEM((2, NSTATE, half), F32),
            pltpu.VMEM((2, 8, half), F32),
            pltpu.VMEM((2, NSTATE + 8, half), F32),
            pltpu.VMEM((NSTATE + 8, half), F32),
            pltpu.VMEM((NSTATE + 8, half), F32),
            pltpu.VMEM((chips, deep + 8, 128), F32),
            pltpu.VMEM((chips, deep + 8, 128), F32),
            pltpu.VMEM((chips, deep, 128), F32),
            pltpu.VMEM((chips, deep, 128), F32),
            pltpu.VMEM((NSTATE, half), F32),
            pltpu.VMEM((NSTATE, half), F32),
            pltpu.VMEM((blocks, 2, NSTATE, half), BF16),
            pltpu.VMEM((chunk, chans), BF16),
            pltpu.VMEM((n_head, PIECES, chunk, width), F32),
            dma((10,)),
            dma((2,)),
            dma((2,)),
            dma((2, chips)),
            dma((2, chips)),
            dma((n_head - 1, PIECES)),
            dma((n_head - 1, PIECES)),
        ]
        return pl.pallas_call(
            functools.partial(kernel, n_ctx, n_head),
            out_shape=jax.ShapeDtypeStruct((chunk, width_out), BF16),
            in_specs=[pl.BlockSpec(memory_space=pl.ANY)] * 10,
            out_specs=pl.BlockSpec(memory_space=pltpu.VMEM),
            scratch_shapes=scratch,
            compiler_params=pltpu.CompilerParams(
                collective_id=0, has_side_effects=True, vmem_limit_bytes=56 * 1024 * 1024
            ),
        )(
            features.reshape(blocks, SPAN, chans),
            gate_values.reshape(blocks, SPAN, chans),
            write_proj.reshape(blocks, SPAN, NSTATE),
            read_proj.reshape(blocks, SPAN, NSTATE),
            step_size,
            log_decay,
            starts.reshape(1, tokens),
            skip_weight.reshape(1, heads),
            norm_gain.reshape(1, chans),
            out_weight,
        )

    placed = (
        P("ctx", "head"),
        P("ctx", "head"),
        P("ctx", "head"),
        P("ctx", "head"),
        P("head", "ctx"),
        P("head", "ctx"),
        P("ctx"),
        P("head"),
        P("head"),
        P("head", None),
    )
    return jax.shard_map(
        body, mesh=mesh, in_specs=placed, out_specs=P(("ctx", "head"), None), check_vma=False
    )
```

time: 539 us -> 110 us (0.20)
  waiting for transfers between devices: 426 us -> 0 us
  Pallas kernels: 0 us -> 108 us
  starting transfers between devices: 59.5 us -> 0 us
  between operations: 13.6 us -> 0.01 us
  matrix products: 12.4 us -> 0 us
  other arithmetic: 12.4 us -> 0 us
  local copies, waits for them, and re-layouts: 11.8 us -> 1.87 us
    ppermute x31 -> x0, waiting for transfers between devices: 331 us -> none  [passed_along(): lax.ppermute(value, axis, [(source, source + steps) for source in range(i...]
    pallas_call x0 -> x1, Pallas kernels: none -> 108 us  [body(): pl.pallas_call(functools.partial(kernel, n_ctx, n_head), out_shape=jax.Sh...]
    reduce_scatter x1 -> x0, waiting for transfers between devices: 95.3 us -> none  [body(): lax.psum_scatter(jnp.dot(normed, out_weight, preferred_element_type=jnp.f...]
    ppermute x31 -> x0, starting transfers between devices: 59.5 us -> none  [passed_along(): lax.ppermute(value, axis, [(source, source + steps) for source in range(i...]
    dot_general x5 -> x0, matrix products: 12.4 us -> none  [the longest x1 7.57 us: body(): jnp.dot(normed, out_weight, preferred_element_type=jnp.float32)]
  transfers between devices with their start and end apart: 32 -> 0, of which waited for: 32 -> 0; matrix products, arithmetic and copies ran while one was open for 0% -> 0% of each run, Pallas kernels for 0% -> 0%
where the time goes in v1:
time: 110 us
  Pallas kernels  108 us (98%)
  local copies, waits for them, and re-layouts  1.87 us (2%)
    pallas_call x1, Pallas kernels, body(): pl.pallas_call(functools.partial(kernel, n_ctx, n_head), out_shape=jax.Sh...  108 us

profile of v1, /device:TPU:6, one launch (start us, length us, event | category | flops | bytes accessed | tf_op | source)
XLA Modules:
  0.0 110.3 jit_solution(6390243245238083339)
XLA Ops:
  0.0 108.5 %shard_map.100 = bf16[64,4096]{1,0:T(8,128)(2,1)} custom-call(bf16[2,256,1024]{2,1,0:T(8,128)(2,1)} %bitcast.7, bf16[2,256,1024]{2,1,0:T(8,128)(2,1)} %bitcast.8, bf16[2,256,128]{2,1,0:T(8,128)(2,1)} %bitcast.9, bf16[2,256,128]{2,1,0:T(8,128)(2,1)} %bitcast.10, f32[16,512]{1,0:T(8,128)} %step_hbm.1, f32[16,512]{1,0:T(8,128)} %decay_hbm.1, ...), custom_call_target="tpu_custom_call" | custom-call | tf_op jit(solution)/shard_map/pallas_call | solution.py:495
  108.5 1.9 %copy.12 = bf16[64,4096]{1,0:T(8,128)(2,1)} copy(bf16[64,4096]{1,0:T(8,128)(2,1)} %shard_map.100) | data formatting | bytes 1048576

commit v2 on v1

--- a/solution.py
+++ b/solution.py
@@ -18,6 +18,7 @@
 MASKED = -1e30
 PIECES = 4
 EARLY = (4, 4)
+FIRST = ("decay", "starts", "step", "write", "feat")
 
 
 def split3(value):
@@ -74,6 +75,7 @@
     entry,
     normed,
     ring,
+    held,
     in_sem,
     pair_send,
     pair_recv,
@@ -96,19 +98,12 @@
     width = ring.shape[3]
     target = lax.rem(z + 1 + (n_head - 2) * core, n_head)
 
-    barrier = pltpu.get_barrier_semaphore()
-    pl.semaphore_signal(barrier, inc=1, device_id={"ctx": other, "head": z}, device_id_type=MESH)
-    for offset in (1, n_head - 1):
-        pl.semaphore_signal(
-            barrier, inc=1, device_id={"ctx": ctx, "head": lax.rem(z + offset, n_head)}, device_id_type=MESH
-        )
-
-    def greet(offset, carry):
-        peer = 2 * lax.rem(chip + offset, chips) + core
-        pl.semaphore_signal(barrier, inc=1, device_id={"ctx": peer, "head": z}, device_id_type=MESH)
-        return carry
-
-    lax.fori_loop(1, chips, greet, 0)
+    side = 4
+    tall = chips // side
+    steps = [(i, j) for i in range(tall) for j in range(side) if (i, j) != (0, 0)]
+    steps.sort(key=lambda step: -min(step[0], tall - step[0]) - min(step[1], side - step[1]))
+    at_x, at_y = chip // side, lax.rem(chip, side)
+    peers = [lax.rem(at_x + i, tall) * side + lax.rem(at_y + j, side) for i, j in steps]
 
     loads = {}
     for index, (name, source, dest) in enumerate(
@@ -126,7 +121,18 @@
         ]
     ):
         loads[name] = pltpu.make_async_copy(source, dest, in_sem.at[index])
-        loads[name].start()
+        if name in FIRST:
+            loads[name].start()
+
+    barrier = pltpu.get_barrier_semaphore()
+    pl.semaphore_signal(barrier, inc=1, device_id={"ctx": other, "head": z}, device_id_type=MESH)
+    for offset in (1, n_head - 1):
+        pl.semaphore_signal(
+            barrier, inc=1, device_id={"ctx": ctx, "head": lax.rem(z + offset, n_head)}, device_id_type=MESH
+        )
+
+    for peer in peers:
+        pl.semaphore_signal(barrier, inc=1, device_id={"ctx": 2 * peer + core, "head": z}, device_id_type=MESH)
 
     row_id = lax.broadcasted_iota(jnp.int32, (span, span), 0)
     col_id = lax.broadcasted_iota(jnp.int32, (span, span), 1)
@@ -167,6 +173,9 @@
         cums.append(cum)
         segs.append(seg)
     loads["feat"].wait()
+    for name, load in loads.items():
+        if name not in FIRST:
+            load.start()
     for k in range(blocks):
         turned = jnp.transpose(write[k].astype(F32))
         write_t[k] = turned.astype(BF16)
@@ -241,24 +250,17 @@
         rows = slice(deep * (q // across), deep * (q // across + 1))
         lanes = slice(128 * (q % across), 128 * (q % across + 1))
         send1[q, :deep] = joined[rows, lanes]
-        send1[q, deep:] = joined_mult[:, lanes]
-
-    def exchange1(offset):
-        peer = lax.rem(chip + offset, chips)
-        return pltpu.make_async_remote_copy(
+        send1[q, deep:] = joined_mult[0:1, lanes]
+
+    for peer in peers:
+        pltpu.make_async_remote_copy(
             src_ref=send1.at[peer],
             dst_ref=recv1.at[chip],
             send_sem=ex_send.at[0, peer],
             recv_sem=ex_recv.at[0, chip],
             device_id={"ctx": 2 * peer + core, "head": z},
             device_id_type=MESH,
-        )
-
-    def start1(offset, carry):
-        exchange1(offset).start()
-        return carry
-
-    lax.fori_loop(1, chips, start1, 0)
+        ).start()
     recv1[chip] = send1[chip]
 
     def chunk_of(s):
@@ -324,26 +326,20 @@
             device_id_type=MESH,
         )
 
-    def scan_step(p, state):
+    for peer in reversed(peers):
+        arrival(0, peer, recv1).wait_recv()
+    state = jnp.zeros((deep, 128), F32)
+    for p in range(chips):
         send2[p] = state
-
-        @pl.when(p != chip)
-        def _():
-            back(p).start()
-            arrival(0, p, recv1).wait_recv()
-
-        return recv1[p, deep : deep + 1] * state + recv1[p, :deep]
-
-    lax.fori_loop(0, chips, scan_step, jnp.zeros((deep, 128), F32))
+        state = recv1[p, deep : deep + 1] * state + recv1[p, :deep]
+    for peer in peers:
+        back(peer).start()
     recv2[chip] = send2[chip]
 
     prepare_loop(EARLY[0], EARLY[0] + EARLY[1])
 
-    def await2(offset, carry):
-        arrival(1, lax.rem(chip + offset, chips), recv2).wait_recv()
-        return carry
-
-    lax.fori_loop(1, chips, await2, 0)
+    for peer in reversed(peers):
+        arrival(1, peer, recv2).wait_recv()
     strips = []
     for down in range(chips // across):
         strips.append(jnp.concatenate([recv2[down * across + right] for right in range(across)], axis=1))
@@ -379,7 +375,7 @@
             device_id_type=MESH,
         )
 
-    def ring_step(s, carry):
+    def normalise(s):
         b = chunk_of(s)
         k = b // per_block
         local = pl.multiple_of(lax.rem(b, per_block) * chunk, chunk)
@@ -396,44 +392,47 @@
         for h in range(2):
             lanes = slice(h * half, (h + 1) * half)
             normed[:, lanes] = (gated[h] * scale * gain[:, lanes]).astype(BF16)
+
+    def product(piece):
+        return jnp.dot(normed[...], weight[:, piece * width : (piece + 1) * width], preferred_element_type=F32)
+
+    def ring_step(s, carry):
+        normalise(s)
         for piece in range(PIECES):
-            lanes = slice(piece * width, (piece + 1) * width)
-            own = jnp.dot(normed[...], weight[:, lanes], preferred_element_type=F32)
+            own = product(piece)
 
             @pl.when(s > 0)
             def _():
                 hop(s - 1, piece).wait_recv()
 
             ring[s, piece] = ring[s, piece] + own
-
-            @pl.when(s < n_head - 1)
-            def _():
-                hop(s, piece).start()
-
-
+            hop(s, piece).start()
         return carry
 
-    lax.fori_loop(0, n_head, ring_step, 0)
+    last = n_head - 1
+    lax.fori_loop(0, last, ring_step, 0)
+    normalise(last)
     for piece in range(PIECES):
-        out_ref[:, piece * width : (piece + 1) * width] = ring[n_head - 1, piece].astype(BF16)
+        held[piece] = product(piece)
 
     pair1.wait_send()
     pair2.wait_send()
-
-    def drain(offset, carry):
-        peer = lax.rem(chip + offset, chips)
+    for peer in peers:
         arrival(0, peer, recv1).wait_send()
         arrival(1, peer, recv2).wait_send()
-        return carry
-
-    lax.fori_loop(1, chips, drain, 0)
-
-    def drain_ring(s, carry):
+
+    def drain(s, carry):
         for piece in range(PIECES):
             hop(s, piece).wait_send()
         return carry
 
-    lax.fori_loop(0, n_head - 1, drain_ring, 0)
+    lax.fori_loop(0, last - 1, drain, 0)
+    for piece in range(PIECES):
+        hop(last - 1, piece).wait_recv()
+        out_ref[:, piece * width : (piece + 1) * width] = (ring[last, piece] + held[piece]).astype(BF16)
+
+    for piece in range(PIECES):
+        hop(last - 1, piece).wait_send()
 
 
 def solution(mesh):
@@ -475,8 +474,8 @@
             pltpu.VMEM((2, NSTATE + 8, half), F32),
             pltpu.VMEM((NSTATE + 8, half), F32),
             pltpu.VMEM((NSTATE + 8, half), F32),
-            pltpu.VMEM((chips, deep + 8, 128), F32),
-            pltpu.VMEM((chips, deep + 8, 128), F32),
+            pltpu.VMEM((chips, deep + 1, 128), F32),
+            pltpu.VMEM((chips, deep + 1, 128), F32),
             pltpu.VMEM((chips, deep, 128), F32),
             pltpu.VMEM((chips, deep, 128), F32),
             pltpu.VMEM((NSTATE, half), F32),
@@ -484,6 +483,7 @@
             pltpu.VMEM((blocks, 2, NSTATE, half), BF16),
             pltpu.VMEM((chunk, chans), BF16),
             pltpu.VMEM((n_head, PIECES, chunk, width), F32),
+            pltpu.VMEM((PIECES, chunk, width), F32),
             dma((10,)),
             dma((2,)),
             dma((2,)),

time: 110 us -> 109 us (level)
    pallas_call x1, Pallas kernels: 108 us -> 107 us  [body(): pl.pallas_call(functools.partial(kernel, n_ctx, n_head), out_shape=jax.Sh...]
where the time goes in v2:
time: 109 us
  Pallas kernels  107 us (98%)
  local copies, waits for them, and re-layouts  1.87 us (2%)
    pallas_call x1, Pallas kernels, body(): pl.pallas_call(functools.partial(kernel, n_ctx, n_head), out_shape=jax.Sh...  107 us

profile of v2, /device:TPU:6, one launch (start us, length us, event | category | flops | bytes accessed | tf_op | source)
XLA Modules:
  0.0 108.6 jit_solution(15921637727836646874)
XLA Ops:
  0.0 106.7 %shard_map.100 = bf16[64,4096]{1,0:T(8,128)(2,1)} custom-call(bf16[2,256,1024]{2,1,0:T(8,128)(2,1)} %bitcast.7, bf16[2,256,1024]{2,1,0:T(8,128)(2,1)} %bitcast.8, bf16[2,256,128]{2,1,0:T(8,128)(2,1)} %bitcast.9, bf16[2,256,128]{2,1,0:T(8,128)(2,1)} %bitcast.10, f32[16,512]{1,0:T(8,128)} %step_hbm.1, f32[16,512]{1,0:T(8,128)} %decay_hbm.1, ...), custom_call_target="tpu_custom_call" | custom-call | tf_op jit(solution)/shard_map/pallas_call | solution.py:495
  106.7 1.9 %copy.12 = bf16[64,4096]{1,0:T(8,128)(2,1)} copy(bf16[64,4096]{1,0:T(8,128)(2,1)} %shard_map.100) | data formatting | bytes 1048576

commit v3 on v2

--- a/solution.py
+++ b/solution.py
@@ -58,6 +58,7 @@
     rows_seg,
     cols,
     expand,
+    expand_tail,
     skip_row,
     ready,
     reach,
@@ -151,6 +152,11 @@
             result = jnp.where(lane_head == i, stacked[i * rows : (i + 1) * rows], result)
         return result
 
+    line = lax.broadcasted_iota(jnp.int32, (NSTATE, chans), 0)
+    owner = lax.broadcasted_iota(jnp.int32, (NSTATE, chans), 1) // HEAD_DIM
+    own_line = lax.rem(line, heads) == owner
+    expand_tail[...] = jnp.where(own_line & (line >= 5 * heads), 1.0, 0.0).astype(BF16)
+
     loads["decay"].wait()
     loads["starts"].wait()
     sums = []
@@ -161,14 +167,19 @@
         sums.append(jnp.dot(stacked, upto, preferred_element_type=F32))
     loads["step"].wait()
     loads["write"].wait()
-    keeps, states, tails, cums, segs = [], [], [], [], []
+    keeps, states, cums, segs = [], [], [], []
     for k in range(blocks):
         tokens = slice(k * span, (k + 1) * span)
         cum = sums[k][0:heads] + sums[k][heads : 2 * heads] + sums[k][2 * heads : 3 * heads]
         seg = sums[k][3 * heads : 3 * heads + 1]
         last = cum[:, span - 1 : span]
         seg_last = seg[:, span - 1 : span]
-        tails.append(jnp.where(seg == seg_last, jnp.exp(last - cum), 0.0) * step[:, tokens])
+        tail = jnp.where(seg == seg_last, jnp.exp(last - cum), 0.0) * step[:, tokens]
+        reach_scale = jnp.where(seg == 0.0, jnp.exp(cum), 0.0)
+        reach_parts = [part.astype(F32) for part in split3(reach_scale)]
+        tail_parts = [part.astype(F32) for part in split3(tail)]
+        seg_rows = jnp.broadcast_to(seg, (heads, span))
+        cols[tokens] = jnp.transpose(jnp.concatenate([cum, *reach_parts, seg_rows, *tail_parts], axis=0))
         keeps.append(spread(jnp.where(seg_last == 0.0, jnp.exp(last), 0.0)))
         cums.append(cum)
         segs.append(seg)
@@ -177,15 +188,14 @@
         if name not in FIRST:
             load.start()
     for k in range(blocks):
-        turned = jnp.transpose(write[k].astype(F32))
-        write_t[k] = turned.astype(BF16)
+        write_t[k] = jnp.transpose(write[k].astype(F32)).astype(BF16)
+        column = cols[k * span : (k + 1) * span].astype(BF16)
         parts = []
         for quad in range(heads // 4):
-            lhs = jnp.concatenate(
-                [(turned * tails[k][4 * quad + i : 4 * quad + i + 1]).astype(BF16) for i in range(4)], axis=0
-            )
-            full = jnp.dot(lhs, feat[k, :, 256 * quad : 256 * (quad + 1)], preferred_element_type=F32)
-            parts.append(diagonal(full, NSTATE))
+            lanes = slice(256 * quad, 256 * (quad + 1))
+            tail = jnp.dot(column, expand_tail[:, lanes], preferred_element_type=F32)
+            scaled = (tail * feat[k, :, lanes].astype(F32)).astype(BF16)
+            parts.append(jnp.dot(write_t[k], scaled, preferred_element_type=F32))
         states.append(parts)
     per_half = half // 256
     for h in range(2):
@@ -209,28 +219,6 @@
         device_id_type=MESH,
     )
     pair1.start()
-
-    def columns_of_block(k):
-        tokens = slice(k * span, (k + 1) * span)
-        rows_u[k] = cums[k] - jnp.log(step[:, tokens])
-        rows_seg[k] = jnp.broadcast_to(segs[k], (8, span))
-        reach_scale = jnp.where(segs[k] == 0.0, jnp.exp(cums[k]), 0.0)
-        pieces = [part.astype(F32) for part in split3(reach_scale)]
-        seg_rows = jnp.broadcast_to(segs[k], (heads, span))
-        pad = jnp.zeros((NSTATE - 5 * heads, span), F32)
-        cols[tokens] = jnp.transpose(jnp.concatenate([cums[k], *pieces, seg_rows, pad], axis=0))
-
-    for k in range(blocks):
-        columns_of_block(k)
-    line = lax.broadcasted_iota(jnp.int32, (NSTATE, chans), 0)
-    owner = lax.broadcasted_iota(jnp.int32, (NSTATE, chans), 1) // HEAD_DIM
-    inside = (line >= heads) & (line < 4 * heads)
-    expand[...] = jnp.where(inside & (lax.rem(line, heads) == owner), 1.0, 0.0).astype(BF16)
-    loads["skip"].wait()
-    square = jnp.broadcast_to(skip[...], (heads, heads))
-    same = lax.broadcasted_iota(jnp.int32, (heads, heads), 0) == lax.broadcasted_iota(jnp.int32, (heads, heads), 1)
-    skip_row[...] = spread(jnp.sum(jnp.where(same, square, 0.0), axis=1, keepdims=True))
-    ring[0] = jnp.zeros_like(ring[0])
 
     pair1.wait_recv()
     mine = total[core]
@@ -262,6 +250,21 @@
             device_id_type=MESH,
         ).start()
     recv1[chip] = send1[chip]
+
+    def rows_of_block(k):
+        tokens = slice(k * span, (k + 1) * span)
+        rows_u[k] = cums[k] - jnp.log(step[:, tokens])
+        rows_seg[k] = jnp.broadcast_to(segs[k], (8, span))
+
+    for k in range(blocks):
+        rows_of_block(k)
+    loads["skip"].wait()
+    square = jnp.broadcast_to(skip[...], (heads, heads))
+    same = lax.broadcasted_iota(jnp.int32, (heads, heads), 0) == lax.broadcasted_iota(jnp.int32, (heads, heads), 1)
+    skip_row[...] = spread(jnp.sum(jnp.where(same, square, 0.0), axis=1, keepdims=True))
+    expand[...] = jnp.where(own_line & (line >= heads) & (line < 4 * heads), 1.0, 0.0).astype(BF16)
+    ring[0] = jnp.zeros_like(ring[0])
+
 
     def chunk_of(s):
         return lax.rem(z + (1 - core) * (n_head - 1 - s) + core * (1 + s), n_head)
@@ -465,6 +468,7 @@
             pltpu.VMEM((blocks, heads, SPAN), F32),
             pltpu.VMEM((blocks, 8, SPAN), F32),
             pltpu.VMEM((tokens, NSTATE), F32),
+            pltpu.VMEM((NSTATE, chans), BF16),
             pltpu.VMEM((NSTATE, chans), BF16),
             pltpu.VMEM((1, chans), F32),
             pltpu.VMEM((n_head, chunk, chans), F32),
@@ -495,23 +499,28 @@
         return pl.pallas_call(
             functools.partial(kernel, n_ctx, n_head),
             out_shape=jax.ShapeDtypeStruct((chunk, width_out), BF16),
-            in_specs=[pl.BlockSpec(memory_space=pl.ANY)] * 10,
+            in_specs=[pl.BlockSpec(memory_space=pltpu.HBM)] * 10,
             out_specs=pl.BlockSpec(memory_space=pltpu.VMEM),
             scratch_shapes=scratch,
             compiler_params=pltpu.CompilerParams(
-                collective_id=0, has_side_effects=True, vmem_limit_bytes=56 * 1024 * 1024
+                collective_id=0, has_side_effects=True, vmem_limit_bytes=48 * 1024 * 1024
             ),
         )(
-            features.reshape(blocks, SPAN, chans),
-            gate_values.reshape(blocks, SPAN, chans),
-            write_proj.reshape(blocks, SPAN, NSTATE),
-            read_proj.reshape(blocks, SPAN, NSTATE),
-            step_size,
-            log_decay,
-            starts.reshape(1, tokens),
-            skip_weight.reshape(1, heads),
-            norm_gain.reshape(1, chans),
-            out_weight,
+            *(
+                pltpu.with_memory_space_constraint(value, pltpu.HBM)
+                for value in (
+                    features.reshape(blocks, SPAN, chans),
+                    gate_values.reshape(blocks, SPAN, chans),
+                    write_proj.reshape(blocks, SPAN, NSTATE),
+                    read_proj.reshape(blocks, SPAN, NSTATE),
+                    step_size,
+                    log_decay,
+                    starts.reshape(1, tokens),
+                    skip_weight.reshape(1, heads),
+                    norm_gain.reshape(1, chans),
+                    out_weight,
+                )
+            )
         )
 
     placed = (

time: 109 us -> 107 us (0.982)
  no operation moved by 1% of the time
where the time goes in v3:
time: 107 us
  Pallas kernels  106 us (99%)
    pallas_call x1, Pallas kernels, body(): pl.pallas_call(functools.partial(kernel, n_ctx, n_head), out_shape=jax.Sh...  106 us

profile of v3, /device:TPU:6, one launch (start us, length us, event | category | flops | bytes accessed | tf_op | source)
XLA Modules:
  0.0 107.0 jit_solution(14976284101922281695)
XLA Ops:
  0.0 106.2 %shard_map.100 = bf16[64,4096]{1,0:T(8,128)(2,1)S(1)} custom-call(bf16[2,256,1024]{2,1,0:T(8,128)(2,1)} %bitcast.7, bf16[2,256,1024]{2,1,0:T(8,128)(2,1)} %bitcast.8, bf16[2,256,128]{2,1,0:T(8,128)(2,1)} %bitcast.9, bf16[2,256,128]{2,1,0:T(8,128)(2,1)} %bitcast.10, f32[16,512]{1,0:T(8,128)} %step_hbm.1, f32[16,512]{1,0:T(8,128)} %decay_hbm.1, ...), custom_call_target="tpu_custom_call" | custom-call | tf_op jit(solution)/shard_map/pallas_call | solution.py:499
  106.2 0.8 copy.12

commit v4 on v3

--- a/solution.py
+++ b/solution.py
@@ -58,7 +58,6 @@
     rows_seg,
     cols,
     expand,
-    expand_tail,
     skip_row,
     ready,
     reach,
@@ -152,11 +151,6 @@
             result = jnp.where(lane_head == i, stacked[i * rows : (i + 1) * rows], result)
         return result
 
-    line = lax.broadcasted_iota(jnp.int32, (NSTATE, chans), 0)
-    owner = lax.broadcasted_iota(jnp.int32, (NSTATE, chans), 1) // HEAD_DIM
-    own_line = lax.rem(line, heads) == owner
-    expand_tail[...] = jnp.where(own_line & (line >= 5 * heads), 1.0, 0.0).astype(BF16)
-
     loads["decay"].wait()
     loads["starts"].wait()
     sums = []
@@ -167,19 +161,14 @@
         sums.append(jnp.dot(stacked, upto, preferred_element_type=F32))
     loads["step"].wait()
     loads["write"].wait()
-    keeps, states, cums, segs = [], [], [], []
+    keeps, states, tails, cums, segs = [], [], [], [], []
     for k in range(blocks):
         tokens = slice(k * span, (k + 1) * span)
         cum = sums[k][0:heads] + sums[k][heads : 2 * heads] + sums[k][2 * heads : 3 * heads]
         seg = sums[k][3 * heads : 3 * heads + 1]
         last = cum[:, span - 1 : span]
         seg_last = seg[:, span - 1 : span]
-        tail = jnp.where(seg == seg_last, jnp.exp(last - cum), 0.0) * step[:, tokens]
-        reach_scale = jnp.where(seg == 0.0, jnp.exp(cum), 0.0)
-        reach_parts = [part.astype(F32) for part in split3(reach_scale)]
-        tail_parts = [part.astype(F32) for part in split3(tail)]
-        seg_rows = jnp.broadcast_to(seg, (heads, span))
-        cols[tokens] = jnp.transpose(jnp.concatenate([cum, *reach_parts, seg_rows, *tail_parts], axis=0))
+        tails.append(jnp.where(seg == seg_last, jnp.exp(last - cum), 0.0) * step[:, tokens])
         keeps.append(spread(jnp.where(seg_last == 0.0, jnp.exp(last), 0.0)))
         cums.append(cum)
         segs.append(seg)
@@ -188,14 +177,15 @@
         if name not in FIRST:
             load.start()
     for k in range(blocks):
-        write_t[k] = jnp.transpose(write[k].astype(F32)).astype(BF16)
-        column = cols[k * span : (k + 1) * span].astype(BF16)
+        turned = jnp.transpose(write[k].astype(F32))
+        write_t[k] = turned.astype(BF16)
         parts = []
         for quad in range(heads // 4):
-            lanes = slice(256 * quad, 256 * (quad + 1))
-            tail = jnp.dot(column, expand_tail[:, lanes], preferred_element_type=F32)
-            scaled = (tail * feat[k, :, lanes].astype(F32)).astype(BF16)
-            parts.append(jnp.dot(write_t[k], scaled, preferred_element_type=F32))
+            lhs = jnp.concatenate(
+                [(turned * tails[k][4 * quad + i : 4 * quad + i + 1]).astype(BF16) for i in range(4)], axis=0
+            )
+            full = jnp.dot(lhs, feat[k, :, 256 * quad : 256 * (quad + 1)], preferred_element_type=F32)
+            parts.append(diagonal(full, NSTATE))
         states.append(parts)
     per_half = half // 256
     for h in range(2):
@@ -251,18 +241,26 @@
         ).start()
     recv1[chip] = send1[chip]
 
-    def rows_of_block(k):
+    def columns_of_block(k):
         tokens = slice(k * span, (k + 1) * span)
         rows_u[k] = cums[k] - jnp.log(step[:, tokens])
         rows_seg[k] = jnp.broadcast_to(segs[k], (8, span))
+        reach_scale = jnp.where(segs[k] == 0.0, jnp.exp(cums[k]), 0.0)
+        pieces = [part.astype(F32) for part in split3(reach_scale)]
+        seg_rows = jnp.broadcast_to(segs[k], (heads, span))
+        pad = jnp.zeros((NSTATE - 5 * heads, span), F32)
+        cols[tokens] = jnp.transpose(jnp.concatenate([cums[k], *pieces, seg_rows, pad], axis=0))
 
     for k in range(blocks):
-        rows_of_block(k)
+        columns_of_block(k)
+    line = lax.broadcasted_iota(jnp.int32, (NSTATE, chans), 0)
+    owner = lax.broadcasted_iota(jnp.int32, (NSTATE, chans), 1) // HEAD_DIM
+    inside = (line >= heads) & (line < 4 * heads)
+    expand[...] = jnp.where(inside & (lax.rem(line, heads) == owner), 1.0, 0.0).astype(BF16)
     loads["skip"].wait()
     square = jnp.broadcast_to(skip[...], (heads, heads))
     same = lax.broadcasted_iota(jnp.int32, (heads, heads), 0) == lax.broadcasted_iota(jnp.int32, (heads, heads), 1)
     skip_row[...] = spread(jnp.sum(jnp.where(same, square, 0.0), axis=1, keepdims=True))
-    expand[...] = jnp.where(own_line & (line >= heads) & (line < 4 * heads), 1.0, 0.0).astype(BF16)
     ring[0] = jnp.zeros_like(ring[0])
 
 
@@ -468,7 +466,6 @@
             pltpu.VMEM((blocks, heads, SPAN), F32),
             pltpu.VMEM((blocks, 8, SPAN), F32),
             pltpu.VMEM((tokens, NSTATE), F32),
-            pltpu.VMEM((NSTATE, chans), BF16),
             pltpu.VMEM((NSTATE, chans), BF16),
             pltpu.VMEM((1, chans), F32),
             pltpu.VMEM((n_head, chunk, chans), F32),

time: 107 us -> 107 us (level)
  no operation moved by 1% of the time
where the time goes in v4:
time: 107 us
  Pallas kernels  106 us (99%)
    pallas_call x1, Pallas kernels, body(): pl.pallas_call(functools.partial(kernel, n_ctx, n_head), out_shape=jax.Sh...  106 us

profile of v4, /device:TPU:6, one launch (start us, length us, event | category | flops | bytes accessed | tf_op | source)
XLA Modules:
  0.0 106.7 jit_solution(11892775633186228377)
XLA Ops:
  0.0 105.9 %shard_map.100 = bf16[64,4096]{1,0:T(8,128)(2,1)S(1)} custom-call(bf16[2,256,1024]{2,1,0:T(8,128)(2,1)} %bitcast.7, bf16[2,256,1024]{2,1,0:T(8,128)(2,1)} %bitcast.8, bf16[2,256,128]{2,1,0:T(8,128)(2,1)} %bitcast.9, bf16[2,256,128]{2,1,0:T(8,128)(2,1)} %bitcast.10, f32[16,512]{1,0:T(8,128)} %step_hbm.1, f32[16,512]{1,0:T(8,128)} %decay_hbm.1, ...), custom_call_target="tpu_custom_call" | custom-call | tf_op jit(solution)/shard_map/pallas_call | solution.py:496
  105.9 0.8 copy.12
